TPU v7x, 32 devices: a whole 2x2x4 slice. The times are simulated.
32 devices in a mesh: parts: 2 (over y), dp: 4 (over z), filt: 4 (over x, core).
Axes of the slice: x: 2, y: 2, z: 4, core: 2. Of those that a mesh axis runs over, the one named last changes fastest.
Arguments:
- inputs: bfloat16 [1008, 8, 576], P('filt', ('parts', 'dp')), parts along dimension 1, may hold values from -6 to 6
- filters: bfloat16 [128, 9, 63, 252], P(('parts', 'dp'), None, None, 'filt'), parts along dimension 0, may hold values from -0.0625 to 0.0625
- out_grad: bfloat16 [1008, 8, 576], P('filt', ('parts', 'dp')), parts along dimension 1, may hold values from -6 to 6
- block_owner: int32 [128], P('parts'), parts along dimension 0, may hold values from 0 to 63, each once
Outputs:
- conv_out: bfloat16 [1008, 8, 576], P('filt', ('parts', 'dp')), parts along dimension 1
- in_grad: bfloat16 [1008, 8, 576], P('filt', ('parts', 'dp')), parts along dimension 1
There are 2 independent parts, one for each index of `parts`. A program takes and returns all parts, laid end to end along the dimension named above; each array names one. Nothing has to cross between parts.
Inputs may be any that keep to these rules, and one draw needn't show every extreme that they name: `block_owner`: each slot holds exactly one block; slots are split evenly and in order along dp.
All inputs are finite; a program needn't handle non-finite values.
Results may differ from a plain program's by a relative error of at most 0.001.
Values may be sent and summed in bfloat16 or wider, within the bound.
A program may use at most 64 MiB of HBM per device.

v0:
```python
import jax
import jax.numpy as jnp
from jax import lax
from jax.sharding import PartitionSpec as P

GW = 1008
HH = 24
WW = 24
CO_SPLIT = 4
CI_SPLIT = 16
CIB = 63


def tap_window(flat, shift_row, shift_col):
    padded = jnp.pad(flat, ((0, 0), (0, 0), (WW + 1, WW + 1)))
    begin = WW + 1 + (shift_row - 1) * WW + (shift_col - 1)
    piece = padded[:, :, begin : begin + HH * WW]
    column = jnp.arange(HH * WW, dtype=jnp.int32) % WW + (shift_col - 1)
    valid = (column >= 0) & (column < WW)
    piece = jnp.where(valid[None, None, :], piece, jnp.zeros_like(piece))
    return piece.reshape(flat.shape[0], flat.shape[1] * HH * WW)


def body(inputs, filters, out_grad, block_owner):
    slot_data = lax.all_gather(filters, "dp", axis=0, tiled=True)
    blocks = jnp.take(slot_data, block_owner, axis=0)
    col_block = filters.shape[3]
    w_local = blocks.reshape(CO_SPLIT, CI_SPLIT, 9, CIB, col_block)
    w_local = w_local.transpose(2, 1, 3, 0, 4).reshape(9, GW, CO_SPLIT * col_block)
    image_total = inputs.shape[1]
    pixel_span = image_total * HH * WW
    start_value = jnp.zeros((w_local.shape[2], pixel_span), jnp.float32)
    running = start_value
    portion = lax.all_gather(inputs, "filt", axis=0, tiled=True)
    for offset in range(9):
        weight_rows = w_local[offset]
        window = tap_window(portion, offset // 3, offset % 3)
        running = running + lax.dot_general(
            weight_rows, window, (((0,), (0,)), ((), ())), preferred_element_type=jnp.float32
        )
    result = running
    conv_out = result.reshape(result.shape[0], image_total, HH * WW).astype(jnp.bfloat16)
    total_sum = jnp.zeros((inputs.shape[0] * lax.axis_size("filt"), pixel_span), jnp.float32)
    for offset in range(9):
        weight_rows = w_local[offset]
        window = tap_window(out_grad, 2 - offset // 3, 2 - offset % 3)
        total_sum = total_sum + jnp.dot(weight_rows, window, preferred_element_type=jnp.float32)
    result = lax.psum_scatter(total_sum, "filt", scatter_dimension=0, tiled=True)
    in_grad = result.reshape(result.shape[0], image_total, HH * WW).astype(jnp.bfloat16)
    return (conv_out, in_grad)


def solution(mesh):
    placed = (
        P("filt", ("parts", "dp"), None),
        P(("parts", "dp"), None, None, "filt"),
        P("filt", ("parts", "dp"), None),
        P("parts"),
    )
    return jax.shard_map(
        body,
        mesh=mesh,
        in_specs=placed,
        out_specs=(P("filt", ("parts", "dp"), None), P("filt", ("parts", "dp"), None)),
        check_vma=False,
    )
```

profile of v0, /device:TPU:1, one launch (start us, length us, event | category | flops | bytes accessed | tf_op | source)
XLA Modules:
  0.0 346.1 jit_solution(12986563329907046966)
XLA Ops:
  7.2 2.0 copy.13
  9.4 0.7 all-gather.3.cloned.1.call-update
  11.5 25.8 %all-gather.5.cloned.1.call-done = bf16[1008,1,576]{2,1,0:T(2,128)(2,1)} async-done(((bf16[252,1,576]{2,1,0:T(2,128)(2,1)}), bf16[1008,1,576]{2,1,0:T(2,128)(2,1)}) %all-gather.5.cloned.1.call-update) | async-done | bytes 1161232 | tf_op jit(solution)/shard_map/all_gather | solution.py:34
  37.3 6.1 %copy.14 = bf16[1008,1,576]{0,2,1:T(8,128)(2,1)} copy(bf16[1008,1,576]{2,1,0:T(2,128)(2,1)} %all-gather.5.cloned.1.call-done) | data formatting | bytes 2322432 | tf_op jit(solution)/shard_map/all_gather | solution.py:34
  43.4 157.5 %all-gather.3.cloned.1.call-done = bf16[64,9,63,63]{3,0,2,1:T(8,128)(2,1)} async-done(((bf16[16,9,63,63]{3,0,2,1:T(8,128)(2,1)}), bf16[64,9,63,63]{3,0,2,1:T(8,128)(2,1)}) %all-gather.3.cloned.1.call-update) | async-done | bytes 4572304 | tf_op jit(solution)/shard_map/all_gather | solution.py:25
  200.8 13.3 %copy.11 = bf16[64,9,63,63]{3,2,1,0:T(8,128)(2,1)} copy(bf16[64,9,63,63]{3,0,2,1:T(8,128)(2,1)} %all-gather.3.cloned.1.call-done) | data formatting | bytes 9144576 | tf_op jit(solution)/shard_map/all_gather | solution.py:25
  214.1 9.8 %gather_fusion = bf16[64,9,63,63]{3,2,1,0:T(8,128)(2,1)} fusion(bf16[64,9,63,63]{3,2,1,0:T(8,128)(2,1)} %copy.11, s32[1024]{0:T(1024)S(1)} %pad_clamp_fusion), kind=kCustom, calls=%fused_computation | custom fusion | bytes 9144832 | tf_op jit(solution)/shard_map/jit(_take)/gather | solution.py:26
  223.9 14.2 %copy.12 = bf16[4,16,9,63,63]{3,1,4,0,2:T(8,128)(2,1)} copy(bf16[4,16,9,63,63]{4,3,2,1,0:T(8,128)(2,1)} %bitcast.120) | data formatting | bytes 9144576 | tf_op jit(solution)/shard_map/jit(_take)/gather | solution.py:26
  238.1 8.2 %select_bitcast_fusion = bf16[9,16,63,4,63]{2,1,4,3,0:T(8,128)(2,1)} fusion(bf16[4,16,9,63,63]{3,1,4,0,2:T(8,128)(2,1)} %copy.12, pred[4,16]{1,0:T(4,128)(4,1)S(1)} %broadcast_in_dim.128), kind=kLoop, calls=%fused_computation.1 | loop fusion | flops 2286144 | bytes 9144640 | tf_op jit(solution)/shard_map/transpose | solution.py:29
  246.3 6.3 %fusion.150 = (bf16[1,16,63,4,63]{2,1,4,3,0:T(8,128)(2,1)}, bf16[1,16,63,4,63]{2,1,4,3,0:T(8,128)(2,1)}, bf16[1,16,63,4,63]{2,1,4,3,0:T(8,128)(2,1)}, bf16[1,16,...) fusion(bf16[9,16,63,4,63]{2,1,4,3,0:T(8,128)(2,1)} %select_bitc, ...), kind=kLoop, calls=%fused_computation.165 | loop fusion | bytes 9144576 | tf_op jit(solution)/shard_map/slice | solution.py:36
  252.6 2.9 squeeze.44
  255.5 2.9 squeeze.43
  258.4 2.9 squeeze.42
  261.3 2.9 squeeze.41
  264.2 2.9 squeeze.40
  267.1 2.9 squeeze.39
  270.0 2.0 squeeze.38
  271.9 1.1 squeeze.37
  273.1 1.1 squeeze.36
  274.2 1.9 fusion.9
  288.1 1.3 fusion.37
  289.3 1.2 add_add_fusion
  290.5 47.9 %all-reduce.4 = bf16[1008,576]{0,1:T(8,128)(2,1)S(1)} all-reduce(f32[1008,576]{0,1:T(8,128)S(1)} %add_add_fusion), channel_id=2, replica_groups=mesh['parts'=2,'dp'=4,'filt'=4] {'filt'}, use_global_device_ids=true, to_apply=%region_0.1.clone | all-reduce | flops 580608 | bytes 3483648
  338.4 0.9 fusion.57
  (48 shorter events, 12.6 us)
Async XLA Ops:
  7.2 30.2 %all-gather.5.cloned.1.call-start = ((), (), s32[]{:S(2)}) async-start(), calls=%async_computation.1 | async-start | bytes 3225600 | tf_op jit(solution)/shard_map/all_gather | solution.py:34
  9.3 0.8 copy-start.9
  9.3 0.9 copy-start.10
  9.3 191.5 %all-gather.3.cloned.1.call-start = ((), (), s32[]{:S(2)}) async-start(), calls=%async_computation | async-start | bytes 11612160 | tf_op jit(solution)/shard_map/all_gather | solution.py:25
  274.2 1.9 copy-start.8
  276.2 1.0 copy-start
  277.6 1.0 copy-start.7
  279.2 1.0 copy-start.6
  280.8 1.0 copy-start.5
  282.3 1.0 copy-start.4
  283.9 1.0 copy-start.3
  285.5 1.0 copy-start.2
  287.0 1.0 copy-start.1
Sparse Core Ops, SparseCore 0:
  9.5 27.7 all-gather.4
  38.9 161.9 all-gather.2
where the time goes:
time: 347 us; the launch traced here: 346 us
  waiting for transfers between devices  184 us (53%)
  local copies, waits for them, and re-layouts  78.6 us (23%)
  blocking collectives  47.9 us (14%)
  between operations  15 us (4%)
  matrix products  12.3 us (4%)
  other arithmetic  8.23 us (2%)
    all_gather x1, waiting for transfers between devices, body(): slot_data = lax.all_gather(filters, 'dp', axis=0, tiled=True)  157 us
    unnamed x1, blocking collectives  47.9 us
    all_gather x1, waiting for transfers between devices, body(): portion = lax.all_gather(inputs, 'filt', axis=0, tiled=True)  25.8 us
    gather x2, local copies, waits for them, and re-layouts, body(): blocks = jnp.take(slot_data, block_owner, axis=0)  24 us
    squeeze x9, local copies, waits for them, and re-layouts, body(): weight_rows = w_local[offset]  21.6 us
    all_gather x1, local copies, waits for them, and re-layouts, body(): slot_data = lax.all_gather(filters, 'dp', axis=0, tiled=True)  13.3 us
    transpose x1, other arithmetic, body(): w_local.transpose(2, 1, 3, 0, 4).reshape(9, GW, CO_SPLIT * col_block)  8.18 us
    dot_general x9, matrix products, body(): lax.dot_general(weight_rows, window, (((0,), (0,)), ((), ())), preferred_...  7.04 us
  transfers between devices with their start and end apart: 2, of which 2 were waited for; matrix products, arithmetic and copies ran while one was open for 2% of the time, Pallas kernels for 0%

commit v1 on v0

v1 whole, which is shorter than its diff:
```python
import functools

import jax
import jax.numpy as jnp
from jax import lax
from jax.experimental import pallas as pl
from jax.experimental.pallas import tpu as pltpu
from jax.sharding import PartitionSpec as P

GW = 1008
HH = 24
WW = 24
CO_SPLIT = 4
CI_SPLIT = 16
CIB = 63
TAPS = 9
SLAB = 64
LANES = 128
MESH = pl.DeviceIdType.MESH
F32 = jnp.float32
BF16 = jnp.bfloat16


def tap_window(flat, shift_row, shift_col):
    padded = jnp.pad(flat, ((0, 0), (0, 0), (WW + 1, WW + 1)))
    begin = WW + 1 + (shift_row - 1) * WW + (shift_col - 1)
    piece = padded[:, :, begin : begin + HH * WW]
    column = jnp.arange(HH * WW, dtype=jnp.int32) % WW + (shift_col - 1)
    valid = (column >= 0) & (column < WW)
    piece = jnp.where(valid[None, None, :], piece, jnp.zeros_like(piece))
    return piece.reshape(flat.shape[0], flat.shape[1] * HH * WW)


def plain_body(inputs, filters, out_grad, block_owner):
    slot_data = lax.all_gather(filters, "dp", axis=0, tiled=True)
    blocks = jnp.take(slot_data, block_owner, axis=0)
    col_block = filters.shape[3]
    w_local = blocks.reshape(CO_SPLIT, CI_SPLIT, TAPS, CIB, col_block)
    w_local = w_local.transpose(2, 1, 3, 0, 4).reshape(TAPS, GW, CO_SPLIT * col_block)
    image_total = inputs.shape[1]
    pixel_span = image_total * HH * WW
    running = jnp.zeros((w_local.shape[2], pixel_span), F32)
    portion = lax.all_gather(inputs, "filt", axis=0, tiled=True)
    for offset in range(TAPS):
        window = tap_window(portion, offset // 3, offset % 3)
        running = running + lax.dot_general(
            w_local[offset], window, (((0,), (0,)), ((), ())), preferred_element_type=F32
        )
    conv_out = running.reshape(running.shape[0], image_total, HH * WW).astype(BF16)
    total_sum = jnp.zeros((inputs.shape[0] * lax.axis_size("filt"), pixel_span), F32)
    for offset in range(TAPS):
        window = tap_window(out_grad, 2 - offset // 3, 2 - offset % 3)
        total_sum = total_sum + jnp.dot(w_local[offset], window, preferred_element_type=F32)
    result = lax.psum_scatter(total_sum, "filt", scatter_dimension=0, tiled=True)
    in_grad = result.reshape(result.shape[0], image_total, HH * WW).astype(BF16)
    return (conv_out, in_grad)


def pack_filters_kernel(f_ref, o_ref):
    half, rows, cols = o_ref.shape[1], f_ref.shape[2], f_ref.shape[3]
    o_ref[...] = jnp.zeros_like(o_ref)
    o_ref[0, :, :rows, :cols] = f_ref[:half, 0]
    o_ref[0, :, :rows, SLAB : SLAB + cols] = f_ref[half:, 0]


def pack_filters(filters):
    slots, taps, rows, cols = filters.shape
    return pl.pallas_call(
        pack_filters_kernel,
        grid=(taps,),
        in_specs=[pl.BlockSpec((slots, 1, rows, cols), lambda t: (0, t, 0, 0))],
        out_specs=pl.BlockSpec((1, slots // 2, SLAB, LANES), lambda t: (t, 0, 0, 0)),
        out_shape=jax.ShapeDtypeStruct((taps, slots // 2, SLAB, LANES), BF16),
    )(filters)


def pack_channels(x, wide):
    slabs = x.shape[0] // CIB
    x = x.reshape(slabs, CIB, x.shape[1] * x.shape[2])
    x = jnp.pad(x, ((0, 0), (0, SLAB - CIB), (0, wide - x.shape[2])))
    return x.reshape(slabs * SLAB, wide)


def main_kernel(
    D, F, w_ref, x_ref, g_ref, idx_ref, half_ref, conv_ref, grad_ref,
    wbuf, cur, xbuf, wt, accb, pair, gathered, summed,
    wsend, wrecv, xsend, xrecv, psend, precv, qsend, qrecv, lsem,
):
    me = lax.axis_index("dp")
    f = lax.axis_index("filt")
    taps, pairs = w_ref.shape[0], w_ref.shape[1]
    rows, wide = x_ref.shape
    core = lax.rem(f, 2)
    chip = f // 2
    G = F // 2

    barrier = pltpu.get_barrier_semaphore()

    @pl.when(me > 0)
    def _():
        pl.semaphore_signal(barrier, inc=1, device_id={"dp": me - 1}, device_id_type=MESH)

    @pl.when(me < D - 1)
    def _():
        pl.semaphore_signal(barrier, inc=1, device_id={"dp": me + 1}, device_id_type=MESH)

    for j in range(1, F):
        pl.semaphore_signal(barrier, inc=1, device_id={"filt": lax.rem(f + j, F)}, device_id_type=MESH)

    def slot(t, o):
        return wbuf.at[t, pl.ds(o * pairs, pairs)]

    own = pltpu.make_async_copy(w_ref, wbuf.at[:, pl.ds(me * pairs, pairs)], lsem.at[0])
    own.start()
    ownx = pltpu.make_async_copy(x_ref, xbuf.at[f], lsem.at[1])
    ownx.start()

    pl.semaphore_wait(barrier, F - 1 + jnp.minimum(me, 1) + jnp.minimum(D - 1 - me, 1))

    def send(src, t, o, side):
        to = me + 1 if side else me - 1
        return pltpu.make_async_remote_copy(
            src_ref=src, dst_ref=slot(t, o), send_sem=wsend.at[side, o, t],
            recv_sem=wrecv.at[o, t], device_id={"dp": to}, device_id_type=MESH,
        )

    def send_own(t):
        @pl.when(me < D - 1)
        def _():
            send(w_ref.at[t], t, me, 1).start()

        @pl.when(me > 0)
        def _():
            send(w_ref.at[t], t, me, 0).start()

    def xcopy(j):
        return pltpu.make_async_remote_copy(
            src_ref=x_ref, dst_ref=xbuf.at[f], send_sem=xsend.at[j],
            recv_sem=xrecv.at[F - j], device_id={"filt": lax.rem(f + j, F)}, device_id_type=MESH,
        )

    LEAD = min(2, taps)
    for t in range(LEAD):
        send_own(t)
    for j in range(1, F):
        xcopy(j).start()
    accb[...] = jnp.zeros_like(accb)
    pix = lax.broadcasted_iota(jnp.int32, (1, wide), 1)
    col = lax.rem(pix, WW)
    gathered[...] = jnp.zeros_like(gathered)
    lane = lax.broadcasted_iota(jnp.int32, (SLAB, LANES), 1)
    own.wait()
    ownx.wait()
    for j in range(1, F):
        pltpu.make_async_remote_copy(
            src_ref=x_ref, dst_ref=xbuf.at[lax.rem(f + j, F)], send_sem=xsend.at[j],
            recv_sem=xrecv.at[j], device_id={"filt": lax.rem(f + j, F)}, device_id_type=MESH,
        ).wait_recv()

    def shifted(value, dr, dc):
        off = dr * WW + dc
        moved = pltpu.roll(value.astype(F32), lax.rem(wide - off, wide), 1)
        good = (col + dc >= 0) & (col + dc < WW)
        return jnp.where(good, moved, 0.0).astype(BF16)

    def assemble(t):
        cur[...] = wbuf[t]

        def one(c, carry):
            for p in range(CO_SPLIT // 2):
                bl, br = (2 * p) * CI_SPLIT + c, (2 * p + 1) * CI_SPLIT + c
                vl = cur[idx_ref[bl]].astype(F32)
                vr = cur[idx_ref[br]].astype(F32)
                left = jnp.where(lane * 0 + half_ref[bl] == 0, vl, pltpu.roll(vl, SLAB, 1))
                right = jnp.where(lane * 0 + half_ref[br] == 1, vr, pltpu.roll(vr, SLAB, 1))
                both = jnp.where(lane < SLAB, left, right).astype(BF16)
                wt[pl.ds(pl.multiple_of(c * SLAB, SLAB), SLAB), p * LANES : (p + 1) * LANES] = both
            return carry

        lax.fori_loop(0, CI_SPLIT, one, 0)

    def backward(t):
        g = shifted(g_ref[...], 1 - t // 3, 1 - lax.rem(t, 3))
        for k in range(F):
            accb[k] += jnp.dot(wt[k * rows : (k + 1) * rows], g, preferred_element_type=F32)

    def forward(t):
        total = gathered[...]
        for k in range(F):
            x = shifted(xbuf[k], t // 3 - 1, lax.rem(t, 3) - 1)
            total += lax.dot_general(
                wt[k * rows : (k + 1) * rows], x, (((0,), (0,)), ((), ())), preferred_element_type=F32
            )
        gathered[...] = total

    def step(t, carry):
        @pl.when(t + LEAD < taps)
        def _():
            send_own(t + LEAD)

        for d in range(1, D):
            @pl.when(me - d >= 0)
            def _():
                send(slot(t, me - d), t, me - d, 1).wait_recv()

                @pl.when(me < D - 1)
                def _():
                    send(slot(t, me - d), t, me - d, 1).start()

            @pl.when(me + d < D)
            def _():
                send(slot(t, me + d), t, me + d, 0).wait_recv()

                @pl.when(me > 0)
                def _():
                    send(slot(t, me + d), t, me + d, 0).start()

        assemble(t)
        backward(t)

        @pl.when(t < taps - 1)
        def _():
            forward(t)

        return carry

    lax.fori_loop(0, taps, step, 0)

    other = chip * 2 + (1 - core)

    def pair_copy(k):
        g = lax.rem(chip + k, G)
        return pltpu.make_async_remote_copy(
            src_ref=accb.at[g * 2 + (1 - core)], dst_ref=pair.at[k], send_sem=psend.at[k],
            recv_sem=precv.at[k], device_id={"filt": other}, device_id_type=MESH,
        )

    def chip_copy(k):
        g = lax.rem(chip + k, G)
        return pltpu.make_async_remote_copy(
            src_ref=summed.at[k], dst_ref=pair.at[G + G - k], send_sem=qsend.at[k],
            recv_sem=qrecv.at[G - k], device_id={"filt": g * 2 + core}, device_id_type=MESH,
        )

    order = list(range(1, G)) + [0]
    for k in order:
        pair_copy(k).start()
    for k in order:
        g = lax.rem(chip + k, G)
        pair_copy(k).wait_recv()
        summed[k] = accb[g * 2 + core] + pair[k]
        if k:
            chip_copy(k).start()
    forward(taps - 1)
    conv_ref[...] = gathered[...].astype(BF16)
    total = summed[0]
    for k in range(1, G):
        chip_copy(k).wait_recv()
        total = total + pair[G + G - k]
    grad_ref[...] = total.astype(BF16)

    for k in range(G):
        pair_copy(k).wait_send()
    for k in range(1, G):
        chip_copy(k).wait_send()
    for j in range(1, F):
        xcopy(j).wait_send()

    def drain(t, carry):
        @pl.when(me < D - 1)
        def _():
            for d in range(D):
                @pl.when(me - d >= 0)
                def _():
                    send(slot(t, me - d), t, me - d, 1).wait_send()

        @pl.when(me > 0)
        def _():
            for d in range(D):
                @pl.when(me + d < D)
                def _():
                    send(slot(t, me + d), t, me + d, 0).wait_send()

        return carry

    lax.fori_loop(0, taps, drain, 0)


def fast_body(D, F, inputs, filters, out_grad, block_owner):
    slots, taps = filters.shape[0], filters.shape[1]
    channels, images, pixels = inputs.shape
    wide = -(-(pixels + WW + 1) // LANES) * LANES
    rows = channels // CIB * SLAB
    pairs = slots // 2
    w = pack_filters(filters)
    x = pack_channels(inputs, wide)
    g = pack_channels(out_grad, wide)
    idx = block_owner // slots * pairs + block_owner % pairs
    half = block_owner % slots // pairs
    G = F // 2
    vm = pl.BlockSpec(memory_space=pltpu.VMEM)
    sm = pl.BlockSpec(memory_space=pltpu.SMEM)
    dma = pltpu.SemaphoreType.DMA
    conv, grad = pl.pallas_call(
        functools.partial(main_kernel, D, F),
        out_shape=[jax.ShapeDtypeStruct((rows, wide), BF16)] * 2,
        in_specs=[vm, vm, vm, sm, sm],
        out_specs=[vm, vm],
        scratch_shapes=[
            pltpu.VMEM((taps, D * pairs, SLAB, LANES), BF16),
            pltpu.VMEM((D * pairs, SLAB, LANES), BF16),
            pltpu.VMEM((F, rows, wide), BF16),
            pltpu.VMEM((F * rows, rows), BF16),
            pltpu.VMEM((F, rows, wide), F32),
            pltpu.VMEM((2 * G, rows, wide), F32),
            pltpu.VMEM((rows, wide), F32),
            pltpu.VMEM((G, rows, wide), F32),
            dma((2, D, taps)), dma((D, taps)), dma((F,)), dma((F,)),
            dma((G,)), dma((G,)), dma((G + 1,)), dma((G + 1,)), dma((2,)),
        ],
        compiler_params=pltpu.CompilerParams(
            collective_id=0, has_side_effects=True, vmem_limit_bytes=60 * 1024 * 1024
        ),
    )(w, x, g, idx, half)

    def unpack(v):
        v = v.reshape(channels // CIB, SLAB, wide)[:, :CIB, :pixels]
        return v.reshape(channels, images, pixels)

    return unpack(conv), unpack(grad)


def solution(mesh):
    D, F = mesh.shape["dp"], mesh.shape["filt"]
    placed = (
        P("filt", ("parts", "dp"), None),
        P(("parts", "dp"), None, None, "filt"),
        P("filt", ("parts", "dp"), None),
        P("parts"),
    )

    def body(inputs, filters, out_grad, block_owner):
        if filters.shape[0] % 2 == 0 and F % 2 == 0 and inputs.shape[1] == 1 and D <= 8:
            return fast_body(D, F, inputs, filters, out_grad, block_owner)
        return plain_body(inputs, filters, out_grad, block_owner)

    return jax.shard_map(
        body,
        mesh=mesh,
        in_specs=placed,
        out_specs=(P("filt", ("parts", "dp"), None), P("filt", ("parts", "dp"), None)),
        check_vma=False,
    )
```

time: 347 us -> 136 us (0.39)
  waiting for transfers between devices: 184 us -> 0 us
  Pallas kernels: 0 us -> 125 us
  local copies, waits for them, and re-layouts: 78.6 us -> 9.79 us
  blocking collectives: 47.9 us -> 0 us
  between operations: 15 us -> 0.67 us
  matrix products: 12.3 us -> 0 us
  other arithmetic: 8.23 us -> 0.53 us
    all_gather x2 -> x0, waiting for transfers between devices: 183 us -> none  [the longest x1 157 us: body(): slot_data = lax.all_gather(filters, 'dp', axis=0, tiled=True)]
    pallas_call x0 -> x2, Pallas kernels: none -> 125 us  [the longest x1 118 us: fast_body(): pl.pallas_call(functools.partial(main_kernel, D, F), out_shape=[jax.Shape...]
    unnamed x1 -> x0, blocking collectives: 47.9 us -> none
    gather x2 -> x0, local copies, waits for them, and re-layouts: 24 us -> none  [body(): blocks = jnp.take(slot_data, block_owner, axis=0)]
    squeeze x9 -> x0, local copies, waits for them, and re-layouts: 21.6 us -> none  [body(): weight_rows = w_local[offset]]
    all_gather x2 -> x0, local copies, waits for them, and re-layouts: 19.3 us -> none  [the longest x1 13.3 us: body(): slot_data = lax.all_gather(filters, 'dp', axis=0, tiled=True)]
    dot_general x18 -> x0, matrix products: 12.3 us -> none  [the longest x9 7.04 us: body(): lax.dot_general(weight_rows, window, (((0,), (0,)), ((), ())), preferred_...]
    transpose x1 -> x0, other arithmetic: 8.18 us -> none  [body(): w_local.transpose(2, 1, 3, 0, 4).reshape(9, GW, CO_SPLIT * col_block)]
  transfers between devices with their start and end apart: 2 -> 0, of which waited for: 2 -> 0; matrix products, arithmetic and copies ran while one was open for 2% -> 0% of each run, Pallas kernels for 0% -> 0%
where the time goes in v1:
time: 136 us; the launch traced here: 135 us
  Pallas kernels  125 us (92%)
  local copies, waits for them, and re-layouts  9.79 us (7%)
    pallas_call x1, Pallas kernels, fast_body(): pl.pallas_call(functools.partial(main_kernel, D, F), out_shape=[jax.Shape...  118 us
    pallas_call x1, Pallas kernels, pack_filters(): pl.pallas_call(pack_filters_kernel, grid=(taps,), in_specs=[pl.BlockSpec(...  6.49 us
    unnamed x11, local copies, waits for them, and re-layouts  5.87 us

profile of v1, /device:TPU:1, one launch (start us, length us, event | category | flops | bytes accessed | tf_op | source)
XLA Modules:
  0.0 135.5 jit_solution(17803868245480869233)
XLA Ops:
  0.6 3.7 %copy.11.f_ref = bf16[16,9,63,63]{3,2,1,0:T(8,128)(2,1)} copy(bf16[16,9,63,63]{3,0,2,1:T(8,128)(2,1)} %param.5) | data formatting | bytes 2286144 | tf_op args[1]
  4.3 0.0 copy-start
  4.3 0.0 copy-start.1
  4.3 6.5 %shard_map.59.w_ref = bf16[9,8,64,128]{3,2,1,0:T(8,128)(2,1)} custom-call(bf16[16,9,63,63]{3,2,1,0:T(8,128)(2,1)} %copy.11.f_ref), custom_call_target="tpu_custom_call" | custom-call | tf_op jit(solution)/shard_map/pallas_call | solution.py:68
  10.8 0.0 copy-done
  10.8 0.0 copy-start.2
  10.8 0.2 copy.12
  11.0 0.1 reshape.28
  11.2 0.7 pad.7
  11.9 0.0 copy-done.1
  11.9 0.2 copy.13
  12.1 0.1 reshape.30
  12.2 0.8 pad.8
  13.0 0.0 copy-done.2
  13.0 0.5 and_select_fusion
  13.5 118.0 %shard_map.60 = (bf16[256,640]{1,0:T(8,128)(2,1)}, bf16[256,640]{1,0:T(8,128)(2,1)}) custom-call(bf16[9,8,64,128]{3,2,1,0:T(8,128)(2,1)} %shard_map.59.w_ref, bf16[256,640]{1,0:T(8,128)(2,1)} %bitcast.10, bf16[256,640]{1,0:T(8,128)(2,1)} %bitcast.11, s32[64]{0:T(128)} %get-tuple-element.9.idx_ref, s32[64]{0:T(128)} %get-tuple-element.8.half_ref), custom_call_target="tpu_custom_call" | custom-call | tf_op jit(solution)/shard_map/pallas_call | solution.py:304
  131.6 1.1 reshape.33
  132.6 0.9 copy.14
  133.5 1.1 reshape.35
  134.6 0.9 copy.15
Async XLA Ops:
  4.3 6.5 %copy-start = (bf16[252,1,576]{0,2,1:T(8,128)(2,1)S(1)}, bf16[252,1,576]{0,2,1:T(8,128)(2,1)}, u32[]{:S(2)}) copy-start(bf16[252,1,576]{0,2,1:T(8,128)(2,1)} %param.4) | copy-start | bytes 870916
  4.3 7.6 %copy-start.1 = (bf16[252,1,576]{0,2,1:T(8,128)(2,1)S(1)}, bf16[252,1,576]{0,2,1:T(8,128)(2,1)}, u32[]{:S(2)}) copy-start(bf16[252,1,576]{0,2,1:T(8,128)(2,1)} %param.6) | copy-start | bytes 870916
  10.8 2.2 %copy-start.2 = (s32[64]{0:T(128)S(1)}, s32[64]{0:T(128)}, u32[]{:S(2)}) copy-start(s32[64]{0:T(128)} %param.7) | copy-start | bytes 772

commit v2 on v1

--- a/solution.py
+++ b/solution.py
@@ -59,37 +59,60 @@
 def pack_filters_kernel(f_ref, o_ref):
     half, rows, cols = o_ref.shape[1], f_ref.shape[2], f_ref.shape[3]
     o_ref[...] = jnp.zeros_like(o_ref)
-    o_ref[0, :, :rows, :cols] = f_ref[:half, 0]
-    o_ref[0, :, :rows, SLAB : SLAB + cols] = f_ref[half:, 0]
+    for t in range(o_ref.shape[0]):
+        o_ref[t, :, :rows, :cols] = f_ref[:half, t]
+        o_ref[t, :, :rows, SLAB : SLAB + cols] = f_ref[half:, t]
 
 
 def pack_filters(filters):
     slots, taps, rows, cols = filters.shape
+    group = 3 if taps % 3 == 0 else 1
     return pl.pallas_call(
         pack_filters_kernel,
-        grid=(taps,),
-        in_specs=[pl.BlockSpec((slots, 1, rows, cols), lambda t: (0, t, 0, 0))],
-        out_specs=pl.BlockSpec((1, slots // 2, SLAB, LANES), lambda t: (t, 0, 0, 0)),
+        grid=(taps // group,),
+        in_specs=[pl.BlockSpec((slots, group, rows, cols), lambda t: (0, t, 0, 0))],
+        out_specs=pl.BlockSpec((group, slots // 2, SLAB, LANES), lambda t: (t, 0, 0, 0)),
         out_shape=jax.ShapeDtypeStruct((taps, slots // 2, SLAB, LANES), BF16),
     )(filters)
 
 
-def pack_channels(x, wide):
-    slabs = x.shape[0] // CIB
-    x = x.reshape(slabs, CIB, x.shape[1] * x.shape[2])
-    x = jnp.pad(x, ((0, 0), (0, SLAB - CIB), (0, wide - x.shape[2])))
-    return x.reshape(slabs * SLAB, wide)
+def pack_channels_kernel(slabs, x_ref, g_ref, xo_ref, go_ref, tmp):
+    pixels, channels = x_ref.shape
+    lane = lax.broadcasted_iota(jnp.int32, tmp.shape, 1)
+    for src, dst in ((x_ref, xo_ref), (g_ref, go_ref)):
+        tmp[...] = jnp.zeros_like(tmp)
+        tmp[:, :channels] = src[...].astype(F32)
+        v = tmp[...]
+        out = jnp.zeros_like(v)
+        for k in range(slabs):
+            moved = v if k == 0 else pltpu.roll(v, k, 1)
+            mine = (lane >= k * SLAB) & (lane < k * SLAB + CIB)
+            out = jnp.where(mine, moved, out)
+        dst[...] = jnp.zeros_like(dst)
+        dst[:pixels] = out.astype(BF16)
+
+
+def pack_channels(x, g, tall, rows):
+    vm = pl.BlockSpec(memory_space=pltpu.VMEM)
+    return pl.pallas_call(
+        functools.partial(pack_channels_kernel, x.shape[1] // CIB),
+        in_specs=[vm, vm],
+        out_specs=[vm, vm],
+        out_shape=[jax.ShapeDtypeStruct((tall, rows), BF16)] * 2,
+        scratch_shapes=[pltpu.VMEM((x.shape[0], rows), F32)],
+    )(x, g)
 
 
 def main_kernel(
     D, F, w_ref, x_ref, g_ref, idx_ref, half_ref, conv_ref, grad_ref,
-    wbuf, cur, xbuf, wt, accb, pair, gathered, summed,
+    wbuf, cur, xbuf, wt, accb, pair, gathered, summed, colbuf,
     wsend, wrecv, xsend, xrecv, psend, precv, qsend, qrecv, lsem,
 ):
     me = lax.axis_index("dp")
     f = lax.axis_index("filt")
     taps, pairs = w_ref.shape[0], w_ref.shape[1]
-    rows, wide = x_ref.shape
+    tall, rows = x_ref.shape
+    pixels, channels = conv_ref.shape
     core = lax.rem(f, 2)
     chip = f // 2
     G = F // 2
@@ -139,28 +162,22 @@
             recv_sem=xrecv.at[F - j], device_id={"filt": lax.rem(f + j, F)}, device_id_type=MESH,
         )
 
-    LEAD = min(2, taps)
+    LEAD = min(4, taps)
     for t in range(LEAD):
         send_own(t)
     for j in range(1, F):
         xcopy(j).start()
     accb[...] = jnp.zeros_like(accb)
-    pix = lax.broadcasted_iota(jnp.int32, (1, wide), 1)
-    col = lax.rem(pix, WW)
+    colbuf[...] = lax.rem(lax.broadcasted_iota(jnp.int32, (tall, rows), 0), WW)
     gathered[...] = jnp.zeros_like(gathered)
     lane = lax.broadcasted_iota(jnp.int32, (SLAB, LANES), 1)
     own.wait()
     ownx.wait()
-    for j in range(1, F):
-        pltpu.make_async_remote_copy(
-            src_ref=x_ref, dst_ref=xbuf.at[lax.rem(f + j, F)], send_sem=xsend.at[j],
-            recv_sem=xrecv.at[j], device_id={"filt": lax.rem(f + j, F)}, device_id_type=MESH,
-        ).wait_recv()
-
     def shifted(value, dr, dc):
         off = dr * WW + dc
-        moved = pltpu.roll(value.astype(F32), lax.rem(wide - off, wide), 1)
-        good = (col + dc >= 0) & (col + dc < WW)
+        moved = pltpu.roll(value.astype(F32), lax.rem(tall - off, tall), 0)
+        col = colbuf[...] + dc
+        good = (col >= 0) & (col < WW)
         return jnp.where(good, moved, 0.0).astype(BF16)
 
     def assemble(t):
@@ -182,15 +199,15 @@
     def backward(t):
         g = shifted(g_ref[...], 1 - t // 3, 1 - lax.rem(t, 3))
         for k in range(F):
-            accb[k] += jnp.dot(wt[k * rows : (k + 1) * rows], g, preferred_element_type=F32)
+            accb[k] += lax.dot_general(
+                g, wt[k * rows : (k + 1) * rows], (((1,), (1,)), ((), ())), preferred_element_type=F32
+            )
 
     def forward(t):
         total = gathered[...]
         for k in range(F):
             x = shifted(xbuf[k], t // 3 - 1, lax.rem(t, 3) - 1)
-            total += lax.dot_general(
-                wt[k * rows : (k + 1) * rows], x, (((0,), (0,)), ((), ())), preferred_element_type=F32
-            )
+            total += jnp.dot(x, wt[k * rows : (k + 1) * rows], preferred_element_type=F32)
         gathered[...] = total
 
     def step(t, carry):
@@ -218,6 +235,14 @@
         assemble(t)
         backward(t)
 
+        @pl.when(t == 0)
+        def _():
+            for j in range(1, F):
+                pltpu.make_async_remote_copy(
+                    src_ref=x_ref, dst_ref=xbuf.at[lax.rem(f + j, F)], send_sem=xsend.at[j],
+                    recv_sem=xrecv.at[j], device_id={"filt": lax.rem(f + j, F)}, device_id_type=MESH,
+                ).wait_recv()
+
         @pl.when(t < taps - 1)
         def _():
             forward(t)
@@ -231,7 +256,7 @@
     def pair_copy(k):
         g = lax.rem(chip + k, G)
         return pltpu.make_async_remote_copy(
-            src_ref=accb.at[g * 2 + (1 - core)], dst_ref=pair.at[k], send_sem=psend.at[k],
+            src_ref=accb.at[g * 2 + (1 - core), pl.ds(0, pixels)], dst_ref=pair.at[k], send_sem=psend.at[k],
             recv_sem=precv.at[k], device_id={"filt": other}, device_id_type=MESH,
         )
 
@@ -248,16 +273,24 @@
     for k in order:
         g = lax.rem(chip + k, G)
         pair_copy(k).wait_recv()
-        summed[k] = accb[g * 2 + core] + pair[k]
+        summed[k] = accb[g * 2 + core, :pixels] + pair[k]
         if k:
             chip_copy(k).start()
     forward(taps - 1)
-    conv_ref[...] = gathered[...].astype(BF16)
+    lanes = lax.broadcasted_iota(jnp.int32, (pixels, rows), 1)
+
+    def closed(v):
+        out = v
+        for k in range(1, channels // CIB):
+            out = jnp.where(lanes >= k * CIB, pltpu.roll(v, rows - k, 1), out)
+        return out.astype(BF16)[:, :channels]
+
+    conv_ref[...] = closed(gathered[:pixels])
     total = summed[0]
     for k in range(1, G):
         chip_copy(k).wait_recv()
         total = total + pair[G + G - k]
-    grad_ref[...] = total.astype(BF16)
+    grad_ref[...] = closed(total)
 
     for k in range(G):
         pair_copy(k).wait_send()
@@ -289,12 +322,11 @@
 def fast_body(D, F, inputs, filters, out_grad, block_owner):
     slots, taps = filters.shape[0], filters.shape[1]
     channels, images, pixels = inputs.shape
-    wide = -(-(pixels + WW + 1) // LANES) * LANES
+    tall = -(-(pixels + WW + 1) // 32) * 32
     rows = channels // CIB * SLAB
     pairs = slots // 2
     w = pack_filters(filters)
-    x = pack_channels(inputs, wide)
-    g = pack_channels(out_grad, wide)
+    x, g = pack_channels(inputs[:, 0].T, out_grad[:, 0].T, tall, rows)
     idx = block_owner // slots * pairs + block_owner % pairs
     half = block_owner % slots // pairs
     G = F // 2
@@ -303,18 +335,19 @@
     dma = pltpu.SemaphoreType.DMA
     conv, grad = pl.pallas_call(
         functools.partial(main_kernel, D, F),
-        out_shape=[jax.ShapeDtypeStruct((rows, wide), BF16)] * 2,
+        out_shape=[jax.ShapeDtypeStruct((pixels, channels), BF16)] * 2,
         in_specs=[vm, vm, vm, sm, sm],
         out_specs=[vm, vm],
         scratch_shapes=[
             pltpu.VMEM((taps, D * pairs, SLAB, LANES), BF16),
             pltpu.VMEM((D * pairs, SLAB, LANES), BF16),
-            pltpu.VMEM((F, rows, wide), BF16),
+            pltpu.VMEM((F, tall, rows), BF16),
             pltpu.VMEM((F * rows, rows), BF16),
-            pltpu.VMEM((F, rows, wide), F32),
-            pltpu.VMEM((2 * G, rows, wide), F32),
-            pltpu.VMEM((rows, wide), F32),
-            pltpu.VMEM((G, rows, wide), F32),
+            pltpu.VMEM((F, tall, rows), F32),
+            pltpu.VMEM((2 * G, pixels, rows), F32),
+            pltpu.VMEM((tall, rows), F32),
+            pltpu.VMEM((G, pixels, rows), F32),
+            pltpu.VMEM((tall, rows), jnp.int32),
             dma((2, D, taps)), dma((D, taps)), dma((F,)), dma((F,)),
             dma((G,)), dma((G,)), dma((G + 1,)), dma((G + 1,)), dma((2,)),
         ],
@@ -323,11 +356,7 @@
         ),
     )(w, x, g, idx, half)
 
-    def unpack(v):
-        v = v.reshape(channels // CIB, SLAB, wide)[:, :CIB, :pixels]
-        return v.reshape(channels, images, pixels)
-
-    return unpack(conv), unpack(grad)
+    return conv.T[:, None], grad.T[:, None]
 
 
 def solution(mesh):

time: 136 us -> 138 us (1.015)
  Pallas kernels: 125 us -> 129 us
  local copies, waits for them, and re-layouts: 9.79 us -> 7.09 us
    pallas_call x1, Pallas kernels: 118 us -> 123 us  [fast_body(): pl.pallas_call(functools.partial(main_kernel, D, F), out_shape=[jax.Shape...]
    reshape x4 -> x0, local copies, waits for them, and re-layouts: 2.4 us -> none  [the longest x2 2.18 us: unpack(): return v.reshape(channels, images, pixels)]
    pad x2 -> x0, local copies, waits for them, and re-layouts: 1.52 us -> none  [pack_channels(): x = jnp.pad(x, ((0, 0), (0, SLAB - CIB), (0, wide - x.shape[2])))]
    unnamed x11 -> x5, local copies, waits for them, and re-layouts: 5.87 us -> 7.09 us
    pallas_call x1 -> x2, Pallas kernels: 6.49 us -> 6.39 us  [the longest x1 3.9 us: pack_filters(): pl.pallas_call(pack_filters_kernel, grid=(taps // group,), in_specs=[pl.B...]
where the time goes in v2:
time: 138 us; the launch traced here: 137 us
  Pallas kernels  129 us (93%)
  local copies, waits for them, and re-layouts  7.09 us (5%)
    pallas_call x1, Pallas kernels, fast_body(): pl.pallas_call(functools.partial(main_kernel, D, F), out_shape=[jax.Shape...  123 us
    unnamed x5, local copies, waits for them, and re-layouts  7.09 us
    pallas_call x1, Pallas kernels, pack_filters(): pl.pallas_call(pack_filters_kernel, grid=(taps // group,), in_specs=[pl.B...  3.9 us

profile of v2, /device:TPU:1, one launch (start us, length us, event | category | flops | bytes accessed | tf_op | source)
XLA Modules:
  0.0 137.4 jit_solution(10382920501769413875)
XLA Ops:
  0.6 3.7 %copy.6.f_ref = bf16[16,9,63,63]{3,2,1,0:T(8,128)(2,1)} copy(bf16[16,9,63,63]{3,0,2,1:T(8,128)(2,1)} %param.5) | data formatting | bytes 2286144 | tf_op args[1]
  4.3 0.0 copy-start
  4.3 3.9 %shard_map.59.w_ref = bf16[9,8,64,128]{3,2,1,0:T(8,128)(2,1)} custom-call(bf16[16,9,63,63]{3,2,1,0:T(8,128)(2,1)} %copy.6.f_ref), custom_call_target="tpu_custom_call" | custom-call | tf_op jit(solution)/shard_map/pallas_call | solution.py:70
  8.2 2.5 %shard_map.60 = (bf16[608,256]{1,0:T(8,128)(2,1)}, bf16[608,256]{1,0:T(8,128)(2,1)}) custom-call(bf16[576,252]{1,0:T(8,128)(2,1)} %bitcast.12, bf16[576,252]{1,0:T(8,128)(2,1)} %bitcast.13), custom_call_target="tpu_custom_call" | custom-call | tf_op jit(solution)/shard_map/pallas_call | solution.py:97
  10.7 0.0 copy-done
  10.7 0.5 and_select_fusion
  11.3 122.7 %shard_map.61 = (bf16[576,252]{1,0:T(8,128)(2,1)}, bf16[576,252]{1,0:T(8,128)(2,1)}) custom-call(bf16[9,8,64,128]{3,2,1,0:T(8,128)(2,1)} %shard_map.59.w_ref, bf16[608,256]{1,0:T(8,128)(2,1)} %get-tuple-element.6.x_ref, bf16[608,256]{1,0:T(8,128)(2,1)} %get-tuple-element.7.g_ref, s32[64]{0:T(128)} %get-tuple-element.11.idx_ref, s32[64]{0:T(128)} %get-tuple-element.10.half_ref), custom_call_target="tpu_custom_call" | custom-call | tf_op jit(solution)/shard_map/pallas_call | solution.py:336
  134.0 1.7 %copy.9 = bf16[252,1,576]{0,2,1:T(8,128)(2,1)} copy(bf16[252,1,576]{0,2,1:T(8,128)(2,1)} %bitcast.15) | data formatting | bytes 580608
  135.7 1.7 %copy.10 = bf16[252,1,576]{0,2,1:T(8,128)(2,1)} copy(bf16[252,1,576]{0,2,1:T(8,128)(2,1)} %bitcast.14) | data formatting | bytes 580608
Async XLA Ops:
  4.3 6.4 %copy-start = (s32[64]{0:T(128)S(1)}, s32[64]{0:T(128)}, u32[]{:S(2)}) copy-start(s32[64]{0:T(128)} %param.7) | copy-start | bytes 772

commit v3 on v2

--- a/solution.py
+++ b/solution.py
@@ -77,7 +77,7 @@
 
 
 def pack_channels_kernel(slabs, x_ref, g_ref, xo_ref, go_ref, tmp):
-    pixels, channels = x_ref.shape
+    channels = x_ref.shape[1]
     lane = lax.broadcasted_iota(jnp.int32, tmp.shape, 1)
     for src, dst in ((x_ref, xo_ref), (g_ref, go_ref)):
         tmp[...] = jnp.zeros_like(tmp)
@@ -88,8 +88,7 @@
             moved = v if k == 0 else pltpu.roll(v, k, 1)
             mine = (lane >= k * SLAB) & (lane < k * SLAB + CIB)
             out = jnp.where(mine, moved, out)
-        dst[...] = jnp.zeros_like(dst)
-        dst[:pixels] = out.astype(BF16)
+        dst[...] = out.astype(BF16)
 
 
 def pack_channels(x, g, tall, rows):
@@ -105,7 +104,7 @@
 
 def main_kernel(
     D, F, w_ref, x_ref, g_ref, idx_ref, half_ref, conv_ref, grad_ref,
-    wbuf, cur, xbuf, wt, accb, pair, gathered, summed, colbuf,
+    wbuf, cur, xbuf, wt, accb, pair, gathered, summed, gsh, xsh,
     wsend, wrecv, xsend, xrecv, psend, precv, qsend, qrecv, lsem,
 ):
     me = lax.axis_index("dp")
@@ -168,17 +167,28 @@
     for j in range(1, F):
         xcopy(j).start()
     accb[...] = jnp.zeros_like(accb)
-    colbuf[...] = lax.rem(lax.broadcasted_iota(jnp.int32, (tall, rows), 0), WW)
     gathered[...] = jnp.zeros_like(gathered)
     lane = lax.broadcasted_iota(jnp.int32, (SLAB, LANES), 1)
     own.wait()
     ownx.wait()
-    def shifted(value, dr, dc):
-        off = dr * WW + dc
-        moved = pltpu.roll(value.astype(F32), lax.rem(tall - off, tall), 0)
-        col = colbuf[...] + dc
-        good = (col >= 0) & (col < WW)
-        return jnp.where(good, moved, 0.0).astype(BF16)
+    col = lax.rem(lax.broadcasted_iota(jnp.int32, (tall, rows), 0), WW)
+
+    def spread(value, dst, lo):
+        v = value.astype(F32)
+        for j in range(3):
+            dc = j - 1
+            moved = v if dc == 0 else pltpu.roll(v, (tall - dc) % tall, 0)
+            good = (col + dc >= 0) & (col + dc < WW)
+            dst[j, WW : WW + tall, lo : lo + rows] = jnp.where(good, moved, 0.0)
+
+    for buf in (gsh, xsh):
+        edge = jnp.zeros((3, WW, buf.shape[2]), F32)
+        buf[:, :WW] = edge
+        buf[:, WW + tall :] = edge
+    spread(g_ref[...], gsh, 0)
+
+    def window(buf, r, c):
+        return buf[c, pl.ds(pl.multiple_of(r * WW, WW), tall)].astype(BF16)
 
     def assemble(t):
         cur[...] = wbuf[t]
@@ -194,21 +204,18 @@
                 wt[pl.ds(pl.multiple_of(c * SLAB, SLAB), SLAB), p * LANES : (p + 1) * LANES] = both
             return carry
 
-        lax.fori_loop(0, CI_SPLIT, one, 0)
+        lax.fori_loop(0, CI_SPLIT, one, 0, unroll=4)
 
     def backward(t):
-        g = shifted(g_ref[...], 1 - t // 3, 1 - lax.rem(t, 3))
+        g = window(gsh, 2 - t // 3, 2 - lax.rem(t, 3))
         for k in range(F):
             accb[k] += lax.dot_general(
                 g, wt[k * rows : (k + 1) * rows], (((1,), (1,)), ((), ())), preferred_element_type=F32
             )
 
     def forward(t):
-        total = gathered[...]
-        for k in range(F):
-            x = shifted(xbuf[k], t // 3 - 1, lax.rem(t, 3) - 1)
-            total += jnp.dot(x, wt[k * rows : (k + 1) * rows], preferred_element_type=F32)
-        gathered[...] = total
+        x = window(xsh, t // 3, lax.rem(t, 3))
+        gathered[...] += jnp.dot(x, wt[...], preferred_element_type=F32)
 
     def step(t, carry):
         @pl.when(t + LEAD < taps)
@@ -242,6 +249,8 @@
                     src_ref=x_ref, dst_ref=xbuf.at[lax.rem(f + j, F)], send_sem=xsend.at[j],
                     recv_sem=xrecv.at[j], device_id={"filt": lax.rem(f + j, F)}, device_id_type=MESH,
                 ).wait_recv()
+            for k in range(F):
+                spread(xbuf[k], xsh, k * rows)
 
         @pl.when(t < taps - 1)
         def _():
@@ -322,7 +331,7 @@
 def fast_body(D, F, inputs, filters, out_grad, block_owner):
     slots, taps = filters.shape[0], filters.shape[1]
     channels, images, pixels = inputs.shape
-    tall = -(-(pixels + WW + 1) // 32) * 32
+    tall = pixels
     rows = channels // CIB * SLAB
     pairs = slots // 2
     w = pack_filters(filters)
@@ -347,7 +356,8 @@
             pltpu.VMEM((2 * G, pixels, rows), F32),
             pltpu.VMEM((tall, rows), F32),
             pltpu.VMEM((G, pixels, rows), F32),
-            pltpu.VMEM((tall, rows), jnp.int32),
+            pltpu.VMEM((3, tall + 2 * WW, rows), F32),
+            pltpu.VMEM((3, tall + 2 * WW, F * rows), F32),
             dma((2, D, taps)), dma((D, taps)), dma((F,)), dma((F,)),
             dma((G,)), dma((G,)), dma((G + 1,)), dma((G + 1,)), dma((2,)),
         ],

time: 138 us -> 118 us (0.86)
  Pallas kernels: 129 us -> 109 us
    pallas_call x1, Pallas kernels: 123 us -> 103 us  [fast_body(): pl.pallas_call(functools.partial(main_kernel, D, F), out_shape=[jax.Shape...]
where the time goes in v3:
time: 118 us
  Pallas kernels  109 us (92%)
  local copies, waits for them, and re-layouts  7.09 us (6%)
    pallas_call x1, Pallas kernels, fast_body(): pl.pallas_call(functools.partial(main_kernel, D, F), out_shape=[jax.Shape...  103 us
    unnamed x5, local copies, waits for them, and re-layouts  7.09 us
    pallas_call x1, Pallas kernels, pack_filters(): pl.pallas_call(pack_filters_kernel, grid=(taps // group,), in_specs=[pl.B...  3.9 us
    pallas_call x1, Pallas kernels, pack_channels(): pl.pallas_call(functools.partial(pack_channels_kernel, x.shape[1] // CIB)...  2.48 us

profile of v3, /device:TPU:1, one launch (start us, length us, event | category | flops | bytes accessed | tf_op | source)
XLA Modules:
  0.0 117.7 jit_solution(40055319146914303)
XLA Ops:
  0.6 3.7 %copy.6.f_ref = bf16[16,9,63,63]{3,2,1,0:T(8,128)(2,1)} copy(bf16[16,9,63,63]{3,0,2,1:T(8,128)(2,1)} %param.5) | data formatting | bytes 2286144 | tf_op args[1]
  4.3 0.0 copy-start
  4.3 3.9 %shard_map.59.w_ref = bf16[9,8,64,128]{3,2,1,0:T(8,128)(2,1)} custom-call(bf16[16,9,63,63]{3,2,1,0:T(8,128)(2,1)} %copy.6.f_ref), custom_call_target="tpu_custom_call" | custom-call | tf_op jit(solution)/shard_map/pallas_call | solution.py:70
  8.2 2.5 %shard_map.60 = (bf16[576,256]{1,0:T(8,128)(2,1)}, bf16[576,256]{1,0:T(8,128)(2,1)}) custom-call(bf16[576,252]{1,0:T(8,128)(2,1)} %bitcast.12, bf16[576,252]{1,0:T(8,128)(2,1)} %bitcast.13), custom_call_target="tpu_custom_call" | custom-call | tf_op jit(solution)/shard_map/pallas_call | solution.py:96
  10.7 0.0 copy-done
  10.7 0.6 and_select_fusion
  11.3 103.0 %shard_map.61 = (bf16[576,252]{1,0:T(8,128)(2,1)}, bf16[576,252]{1,0:T(8,128)(2,1)}) custom-call(bf16[9,8,64,128]{3,2,1,0:T(8,128)(2,1)} %shard_map.59.w_ref, bf16[576,256]{1,0:T(8,128)(2,1)} %get-tuple-element.6.x_ref, bf16[576,256]{1,0:T(8,128)(2,1)} %get-tuple-element.7.g_ref, s32[64]{0:T(128)} %get-tuple-element.11.idx_ref, s32[64]{0:T(128)} %get-tuple-element.10.half_ref), custom_call_target="tpu_custom_call" | custom-call | tf_op jit(solution)/shard_map/pallas_call | solution.py:345
  114.3 1.7 %copy.9 = bf16[252,1,576]{0,2,1:T(8,128)(2,1)} copy(bf16[252,1,576]{0,2,1:T(8,128)(2,1)} %bitcast.15) | data formatting | bytes 580608
  116.0 1.7 %copy.10 = bf16[252,1,576]{0,2,1:T(8,128)(2,1)} copy(bf16[252,1,576]{0,2,1:T(8,128)(2,1)} %bitcast.14) | data formatting | bytes 580608
Async XLA Ops:
  4.3 6.4 %copy-start = (s32[64]{0:T(128)S(1)}, s32[64]{0:T(128)}, u32[]{:S(2)}) copy-start(s32[64]{0:T(128)} %param.7) | copy-start | bytes 772

commit v4 on v3

--- a/solution.py
+++ b/solution.py
@@ -76,42 +76,16 @@
     )(filters)
 
 
-def pack_channels_kernel(slabs, x_ref, g_ref, xo_ref, go_ref, tmp):
-    channels = x_ref.shape[1]
-    lane = lax.broadcasted_iota(jnp.int32, tmp.shape, 1)
-    for src, dst in ((x_ref, xo_ref), (g_ref, go_ref)):
-        tmp[...] = jnp.zeros_like(tmp)
-        tmp[:, :channels] = src[...].astype(F32)
-        v = tmp[...]
-        out = jnp.zeros_like(v)
-        for k in range(slabs):
-            moved = v if k == 0 else pltpu.roll(v, k, 1)
-            mine = (lane >= k * SLAB) & (lane < k * SLAB + CIB)
-            out = jnp.where(mine, moved, out)
-        dst[...] = out.astype(BF16)
-
-
-def pack_channels(x, g, tall, rows):
-    vm = pl.BlockSpec(memory_space=pltpu.VMEM)
-    return pl.pallas_call(
-        functools.partial(pack_channels_kernel, x.shape[1] // CIB),
-        in_specs=[vm, vm],
-        out_specs=[vm, vm],
-        out_shape=[jax.ShapeDtypeStruct((tall, rows), BF16)] * 2,
-        scratch_shapes=[pltpu.VMEM((x.shape[0], rows), F32)],
-    )(x, g)
-
-
 def main_kernel(
     D, F, w_ref, x_ref, g_ref, idx_ref, half_ref, conv_ref, grad_ref,
-    wbuf, cur, xbuf, wt, accb, pair, gathered, summed, gsh, xsh,
+    wbuf, cur, xbuf, wt, accb, pair, gathered, summed, gsh, xsh, tmp,
     wsend, wrecv, xsend, xrecv, psend, precv, qsend, qrecv, lsem,
 ):
     me = lax.axis_index("dp")
     f = lax.axis_index("filt")
     taps, pairs = w_ref.shape[0], w_ref.shape[1]
-    tall, rows = x_ref.shape
-    pixels, channels = conv_ref.shape
+    tall, channels = x_ref.shape
+    pixels, rows = tall, wt.shape[1]
     core = lax.rem(f, 2)
     chip = f // 2
     G = F // 2
@@ -173,8 +147,17 @@
     ownx.wait()
     col = lax.rem(lax.broadcasted_iota(jnp.int32, (tall, rows), 0), WW)
 
+    chan = lax.broadcasted_iota(jnp.int32, (tall, rows), 1)
+    tmp[...] = jnp.zeros_like(tmp)
+
     def spread(value, dst, lo):
-        v = value.astype(F32)
+        tmp[:, :channels] = value.astype(F32)
+        raw = tmp[...]
+        v = jnp.zeros_like(raw)
+        for k in range(channels // CIB):
+            moved = raw if k == 0 else pltpu.roll(raw, k, 1)
+            mine = (chan >= k * SLAB) & (chan < k * SLAB + CIB)
+            v = jnp.where(mine, moved, v)
         for j in range(3):
             dc = j - 1
             moved = v if dc == 0 else pltpu.roll(v, (tall - dc) % tall, 0)
@@ -335,7 +318,7 @@
     rows = channels // CIB * SLAB
     pairs = slots // 2
     w = pack_filters(filters)
-    x, g = pack_channels(inputs[:, 0].T, out_grad[:, 0].T, tall, rows)
+    x, g = inputs[:, 0].T, out_grad[:, 0].T
     idx = block_owner // slots * pairs + block_owner % pairs
     half = block_owner % slots // pairs
     G = F // 2
@@ -350,7 +333,7 @@
         scratch_shapes=[
             pltpu.VMEM((taps, D * pairs, SLAB, LANES), BF16),
             pltpu.VMEM((D * pairs, SLAB, LANES), BF16),
-            pltpu.VMEM((F, tall, rows), BF16),
+            pltpu.VMEM((F, tall, channels), BF16),
             pltpu.VMEM((F * rows, rows), BF16),
             pltpu.VMEM((F, tall, rows), F32),
             pltpu.VMEM((2 * G, pixels, rows), F32),
@@ -358,6 +341,7 @@
             pltpu.VMEM((G, pixels, rows), F32),
             pltpu.VMEM((3, tall + 2 * WW, rows), F32),
             pltpu.VMEM((3, tall + 2 * WW, F * rows), F32),
+            pltpu.VMEM((tall, rows), F32),
             dma((2, D, taps)), dma((D, taps)), dma((F,)), dma((F,)),
             dma((G,)), dma((G,)), dma((G + 1,)), dma((G + 1,)), dma((2,)),
         ],

time: 118 us -> 116 us (0.983)
    pallas_call x1 -> x0, Pallas kernels: 2.48 us -> none  [pack_channels(): pl.pallas_call(functools.partial(pack_channels_kernel, x.shape[1] // CIB)...]
where the time goes in v4:
time: 116 us
  Pallas kernels  108 us (93%)
  local copies, waits for them, and re-layouts  7.09 us (6%)
    pallas_call x1, Pallas kernels, fast_body(): pl.pallas_call(functools.partial(main_kernel, D, F), out_shape=[jax.Shape...  104 us
    unnamed x5, local copies, waits for them, and re-layouts  7.09 us
    pallas_call x1, Pallas kernels, pack_filters(): pl.pallas_call(pack_filters_kernel, grid=(taps // group,), in_specs=[pl.B...  3.89 us

profile of v4, /device:TPU:1, one launch (start us, length us, event | category | flops | bytes accessed | tf_op | source)
XLA Modules:
  0.0 116.1 jit_solution(11651331069726628705)
XLA Ops:
  0.6 3.7 %copy.6.f_ref = bf16[16,9,63,63]{3,2,1,0:T(8,128)(2,1)} copy(bf16[16,9,63,63]{3,0,2,1:T(8,128)(2,1)} %param.5) | data formatting | bytes 2286144 | tf_op args[1]
  4.3 0.0 copy-start
  4.3 3.9 %shard_map.59.w_ref = bf16[9,8,64,128]{3,2,1,0:T(8,128)(2,1)} custom-call(bf16[16,9,63,63]{3,2,1,0:T(8,128)(2,1)} %copy.6.f_ref), custom_call_target="tpu_custom_call" | custom-call | tf_op jit(solution)/shard_map/pallas_call | solution.py:70
  8.2 0.0 copy-done
  8.2 0.5 and_select_fusion
  8.7 104.0 %shard_map.60 = (bf16[576,252]{1,0:T(8,128)(2,1)}, bf16[576,252]{1,0:T(8,128)(2,1)}) custom-call(bf16[9,8,64,128]{3,2,1,0:T(8,128)(2,1)} %shard_map.59.w_ref, bf16[576,252]{1,0:T(8,128)(2,1)} %bitcast.14, bf16[576,252]{1,0:T(8,128)(2,1)} %bitcast.15, s32[64]{0:T(128)} %get-tuple-element.7.idx_ref, s32[64]{0:T(128)} %get-tuple-element.6.half_ref), custom_call_target="tpu_custom_call" | custom-call | tf_op jit(solution)/shard_map/pallas_call | solution.py:328
  112.7 1.7 %copy.9 = bf16[252,1,576]{0,2,1:T(8,128)(2,1)} copy(bf16[252,1,576]{0,2,1:T(8,128)(2,1)} %bitcast.13) | data formatting | bytes 580608
  114.4 1.7 %copy.10 = bf16[252,1,576]{0,2,1:T(8,128)(2,1)} copy(bf16[252,1,576]{0,2,1:T(8,128)(2,1)} %bitcast.12) | data formatting | bytes 580608
Async XLA Ops:
  4.3 3.9 %copy-start = (s32[64]{0:T(128)S(1)}, s32[64]{0:T(128)}, u32[]{:S(2)}) copy-start(s32[64]{0:T(128)} %param.7) | copy-start | bytes 772
